TPU v7x, 256 devices: a whole 4x4x8 slice. The times are simulated.
256 devices in a mesh: rep: 16 (over z, core), row: 4 (over y), col: 4 (over x).
Axes of the slice: x: 4, y: 4, z: 8, core: 2. Of those that a mesh axis runs over, the one named last changes fastest.
Arguments:
- hidden_in: bfloat16 [16384, 2048], P(('rep', 'row', 'col')), may hold values from -6 to 6
- w_qkv: bfloat16 [2048, 16, 384], P(None, ('row', 'col')), may hold values from -0.125 to 0.125
- w_out: bfloat16 [16, 128, 2048], P(('row', 'col')), may hold values from -0.5 to 0.5
- w_gate_up: bfloat16 [2048, 2, 8192], P(None, None, ('row', 'col')), may hold values from -0.125 to 0.125
- w_down: bfloat16 [8192, 2048], P(('row', 'col')), may hold values from -0.0625 to 0.0625
- cache: bfloat16 [128, 2, 256, 16, 128], P('rep', None, None, ('row', 'col'))
- span_len: int32 [128], replicated, may hold values from 1 to 128, 8192 in all
- cache_len: int32 [128], replicated, may hold values from 1 to 256, 16384 in all
- new_slot: int32 [128], replicated, may hold values from 0 to 127, as said below
Outputs:
- hidden_out: bfloat16 [16384, 2048], P(('rep', 'row', 'col'))
- cache_out: bfloat16 [128, 2, 384, 16, 128], P('rep', None, None, ('row', 'col'))
Inputs may be any that keep to these rules, and one draw needn't show every extreme that they name: A permutation of the 128 slots; slot s lies on replica s // 8, and new_slot[r] mod 8 equals r mod 8; the 8 requests of one replica go to at most 1 slots of any one replica, and some pair of replicas has exactly 1.
All inputs are finite; a program needn't handle non-finite values.
Results may differ from a plain program's by a relative error of at most 0.014.
The roundings to bfloat16 on the way count: a program that leaves them out, or rounds other values in their place, can miss the bound.
Values may be sent and summed in bfloat16 or wider, within the bound.
No kernel may reach another device: no remote copies, remote signals or barrier semaphores. Data moves between devices by JAX's collectives and lax.ppermute only.
A program may use at most 128 MiB of HBM per device.

v0:
```python
import math
import jax
import jax.numpy as jnp
from jax import lax
from jax.sharding import PartitionSpec as P

EPSILON = 1e-05


def layer_norm(values):
    centred = values - jnp.mean(values, axis=-1, keepdims=True)
    spread = jnp.mean(centred * centred, axis=-1, keepdims=True)
    return centred * lax.rsqrt(spread + EPSILON)


def rotate(values, positions):
    halfway = values.shape[-1] // 2
    frequency = 10000.0 ** (-(jnp.arange(halfway, dtype=jnp.float32) * 2.0 / values.shape[-1]))
    angles = positions[..., None] * frequency
    cosine = jnp.cos(angles)
    sine_part = jnp.sin(angles)
    first_half = values[..., :halfway]
    second_half = values[..., halfway:]
    return jnp.concatenate(
        [
            first_half * cosine - second_half * sine_part,
            second_half * cosine + first_half * sine_part,
        ],
        axis=-1,
    )


def attend_one(queries, keys_new, values_new, cache_old, length_old):
    total_keys = jnp.concatenate([cache_old[0], keys_new], axis=0)
    total_values = jnp.concatenate([cache_old[1], values_new], axis=0)
    scores = jnp.einsum("thd,shd->hts", queries, total_keys, preferred_element_type=jnp.float32) * (
        1.0 / math.sqrt(queries.shape[-1])
    )
    source_pos = jnp.arange(total_keys.shape[0], dtype=jnp.int32)
    query_pos = jnp.arange(queries.shape[0], dtype=jnp.int32)
    stored = cache_old.shape[1]
    allowed = jnp.where(
        source_pos[None, :] < stored,
        source_pos[None, :] < length_old,
        source_pos[None, :] - stored <= query_pos[:, None],
    )
    masked_scores = jnp.where(allowed[None], scores, -1e30)
    highest = jnp.max(masked_scores, axis=-1, keepdims=True)
    exponent = jnp.where(allowed[None], jnp.exp(masked_scores - highest), 0.0)
    weights = (exponent / jnp.sum(exponent, axis=-1, keepdims=True)).astype(jnp.bfloat16)
    return jnp.einsum(
        "hts,shd->thd", weights, total_values, preferred_element_type=jnp.float32
    ).astype(jnp.bfloat16)


def assemble_one(old_rows, new_rows, length_old):
    zero_index = jnp.zeros((), jnp.int32)
    extended = jnp.concatenate([old_rows, jnp.zeros_like(new_rows)], axis=1)
    placed = lax.dynamic_update_slice(
        jnp.zeros_like(extended), new_rows, (zero_index, length_old, zero_index, zero_index)
    )
    return extended + placed


def route_tables(new_slot, replica, replicas, slot_count, capacity):
    request_ids = jnp.arange(new_slot.shape[0], dtype=jnp.int32)
    owners = request_ids // slot_count
    targets = new_slot // slot_count
    same_group = (
        (owners[:, None] == owners[None, :])
        & (targets[:, None] == targets[None, :])
        & (request_ids[None, :] < request_ids[:, None])
    )
    ranks = jnp.sum(same_group.astype(jnp.int32), axis=1)
    my_targets = lax.dynamic_slice_in_dim(targets, replica * slot_count, slot_count)
    my_ranks = lax.dynamic_slice_in_dim(ranks, replica * slot_count, slot_count)
    entries = jnp.arange(replicas * capacity, dtype=jnp.int32)
    matches = (my_targets[None, :] == (entries // capacity)[:, None]) & (
        my_ranks[None, :] == (entries % capacity)[:, None]
    )
    send_from = jnp.sum(
        matches.astype(jnp.int32) * jnp.arange(slot_count, dtype=jnp.int32)[None, :], axis=1
    )
    send_live = jnp.any(matches, axis=1)
    my_slots = replica * slot_count + jnp.arange(slot_count, dtype=jnp.int32)
    arrivals = (new_slot[None, :] == my_slots[:, None]).astype(jnp.int32)
    recv_index = jnp.sum(arrivals * (owners * capacity + ranks)[None, :], axis=1)
    return (send_from, send_live, recv_index, arrivals)


def pack_rows(stacked, send_from, send_live):
    taken_rows = jnp.take(stacked, send_from, axis=0)
    live_shape = send_live.reshape((send_live.shape[0],) + (1,) * (stacked.ndim - 1))
    return jnp.where(live_shape, taken_rows, 0.0)


def body(hidden_in, w_qkv, w_out, w_gate_up, w_down, cache, span_len, cache_len, new_slot):
    slot_count = cache.shape[0]
    stored = cache.shape[2]
    heads_here = cache.shape[3]
    head_size = cache.shape[4]
    model_width = hidden_in.shape[1]
    local_rows = hidden_in.shape[0]
    ff_here = w_down.shape[0]
    replica = lax.axis_index("rep")
    replicas = lax.axis_size("rep")
    capacity = (slot_count + replicas - 1) // replicas
    my_cached = lax.dynamic_slice_in_dim(cache_len, replica * slot_count, slot_count)
    my_spans = lax.dynamic_slice_in_dim(span_len, replica * slot_count, slot_count)
    send_from, send_live, recv_index, arrivals = route_tables(
        new_slot, replica, replicas, slot_count, capacity
    )
    stored_rows = jnp.arange(stored, dtype=jnp.int32)
    old_kept = jnp.where(
        (stored_rows[None, :] < my_cached[:, None])[:, None, :, None, None], cache, 0.0
    )
    inputs = hidden_in.astype(jnp.float32)
    normed = layer_norm(inputs).astype(jnp.bfloat16)
    joined = jnp.dot(
        lax.all_gather(normed, ("row", "col"), axis=0, tiled=True),
        w_qkv.reshape(model_width, heads_here * 3 * head_size),
        preferred_element_type=jnp.float32,
    )
    span_rows = joined.shape[0] // slot_count
    joined = joined.reshape(slot_count, span_rows, heads_here, 3, head_size)
    offsets = jnp.arange(span_rows, dtype=jnp.int32)
    positions = (my_cached[:, None] + offsets[None, :]).astype(jnp.float32)[:, :, None]
    queries = rotate(joined[:, :, :, 0], positions).astype(jnp.bfloat16)
    keys_new = rotate(joined[:, :, :, 1], positions).astype(jnp.bfloat16)
    values_new = joined[:, :, :, 2].astype(jnp.bfloat16)
    context = jax.vmap(attend_one)(queries, keys_new, values_new, old_kept, my_cached)
    flat_context = context.reshape(slot_count * span_rows, heads_here * head_size)
    picked = flat_context
    attention = lax.psum_scatter(
        jnp.dot(
            picked,
            w_out.reshape(heads_here * head_size, model_width),
            preferred_element_type=jnp.float32,
        ),
        ("row", "col"),
        scatter_dimension=0,
        tiled=True,
    )
    new_kv = jnp.stack([keys_new, values_new], axis=1)
    new_kept = jnp.where(
        (offsets[None, :] < my_spans[:, None])[:, None, :, None, None], new_kv, 0.0
    )
    appended = jax.vmap(assemble_one)(old_kept, new_kept, my_cached)
    moved_rows = lax.all_to_all(
        pack_rows(appended, send_from, send_live), "rep", split_axis=0, concat_axis=0, tiled=True
    )
    cache_out = jnp.take(moved_rows, recv_index, axis=0)
    middle = (inputs + attention).astype(jnp.bfloat16)
    normed_mid = layer_norm(middle.astype(jnp.float32)).astype(jnp.bfloat16)
    gate_up = jnp.dot(
        lax.all_gather(normed_mid, ("row", "col"), axis=0, tiled=True),
        w_gate_up.reshape(model_width, 2 * ff_here),
        preferred_element_type=jnp.float32,
    )
    hidden = (jax.nn.silu(gate_up[:, :ff_here]) * gate_up[:, ff_here:]).astype(jnp.bfloat16)
    picked = hidden
    down_sum = lax.psum_scatter(
        jnp.dot(picked, w_down, preferred_element_type=jnp.float32).astype(jnp.bfloat16),
        ("row", "col"),
        scatter_dimension=0,
        tiled=True,
    ).astype(jnp.float32)
    row_ids = lax.axis_index(("row", "col")) * local_rows + jnp.arange(local_rows, dtype=jnp.int32)
    slot_of = row_ids // span_rows
    within = row_ids % span_rows
    lengths = jnp.sum(
        jnp.where(
            slot_of[:, None] == jnp.arange(slot_count, dtype=jnp.int32)[None, :],
            my_spans[None, :],
            0,
        ),
        axis=1,
    )
    hidden_out = jnp.where(
        (within < lengths)[:, None], middle.astype(jnp.float32) + down_sum, 0.0
    ).astype(jnp.bfloat16)
    return (hidden_out, cache_out)


def solution(mesh):
    in_specs = (
        P(("rep", "row", "col"), None),
        P(None, ("row", "col"), None),
        P(("row", "col"), None, None),
        P(None, None, ("row", "col")),
        P(("row", "col"), None),
        P("rep", None, None, ("row", "col"), None),
        P(),
        P(),
        P(),
    )
    out_specs = (P(("rep", "row", "col"), None), P("rep", None, None, ("row", "col"), None))
    return jax.shard_map(body, mesh=mesh, in_specs=in_specs, out_specs=out_specs, check_vma=False)
```

profile of v0, /device:TPU:1, one launch (start us, length us, event | category | flops | bytes accessed | tf_op | source)
XLA Modules:
  0.0 450.9 jit_solution(6191463887724648742)
XLA Ops:
  18.2 53.8 %all-gather.3.cloned.1.call-done = bf16[1024,2048]{1,0:T(8,128)(2,1)} async-done(((bf16[64,2048]{1,0:T(8,128)(2,1)}), bf16[1024,2048]{1,0:T(8,128)(2,1)}) %all-gather.3.cloned.1.call-update) | async-done | bytes 4194320 | tf_op jit(solution)/shard_map/all_gather | solution.py:120
  72.0 4.1 convolution_bitcast_fusion
  83.2 3.2 fusion.71
  88.6 4.5 fusion.24
  93.1 88.8 %reduce-scatter.3.cloned.1.call-done = f32[64,2048]{1,0:T(8,128)} async-done(((f32[1024,2048]{1,0:T(8,128)}), f32[64,2048]{1,0:T(8,128)}) %reduce-scatter.3.cloned.1.call-update) | async-done | bytes 524304 | tf_op jit(solution)/shard_map/reduce_scatter | solution.py:134
  185.9 5.4 %copy.76 = bf16[256,8,2,512]{3,1,2,0:T(8,128)(2,1)} copy(bf16[256,8,2,512]{3,2,1,0:T(2,128)(2,1)} %bitcast.121) | data formatting | bytes 8388608
  194.1 48.1 %all-gather.5.cloned.1.call-done = bf16[1024,2048]{1,0:T(8,128)(2,1)} async-done(((bf16[64,2048]{1,0:T(8,128)(2,1)}), bf16[1024,2048]{1,0:T(8,128)(2,1)}) %all-gather.5.cloned.1.call-update) | async-done | bytes 4194320 | tf_op jit(solution)/shard_map/all_gather | solution.py:156
  242.2 7.5 %fusion.74 = f32[1024,1024]{1,0:T(8,128)S(1)} fusion(bf16[1024,2048]{1,0:T(8,128)(2,1)} %all-gather.5.cloned.1.call-done, bf16[2048,1024]{1,0:T(8,128)(2,1)} %bitcast.122), kind=kOutput, calls=%fused_computation.147 | convolution fusion | flops 4294967296 | bytes 12582912 | tf_op jit(solution)/shard_map/dot_general | solution.py:155
  249.7 4.3 convolution_convert_fusion
  255.5 90.9 %while.1 = (s32[]{:T(128)}, bf16[8,2,384,1,128]{4,2,0,3,1:T(8,128)(2,1)}, s32[8,5]{1,0:T(8,128)S(1)}, bf16[8,2,128,1,128]{2,4,0,3,1:T(8,128)(2,1)}, s32[]{:T(128)}, /*index=5*/s32[5]{0:T(128)S(1)}, s32[]{:T(128)}) while((s32[]{:T(128)}, bf16[8,2,384,1,128]{4,2,0,3,1:T(8,128)(2,1)}, s32[8,5]{1,0:T(8,128)S(1)}, bf16[8,2,128,1,128]{2,4,0,3,1:T(8,128)(2,1)}, ...), condition=%wide.while_cond, body=%wide.while_body.sunk | while | flops 32789 | bytes 852227 | solution.py:59
  256.2 3.2 concatenate.79
  264.0 2.9 dynamic-update-slice.3
  267.6 3.2 concatenate.79
  278.9 3.2 concatenate.79
  290.3 3.2 concatenate.79
  301.7 3.2 concatenate.79
  313.0 3.2 concatenate.79
  324.4 3.2 concatenate.79
  335.7 3.2 concatenate.79
  349.3 4.1 gather_fusion
  353.4 4.0 fusion.2
  357.5 7.5 %all-to-all-start = ((bf16[16,2,384,1,128]{4,2,1,3,0:T(8,128)(2,1)}), bf16[16,2,384,1,128]{4,2,1,3,0:T(8,128)(2,1)}, u32[]{:S(2)}, u32[]{:S(2)}) async-start(bf16[16,2,384,1,128]{4,2,1,3,0:T(8,128)(2,1)} %fusion.2), calls=%async_computation.2 | async-start | bytes 6291456 | tf_op jit(solution)/shard_map/all_to_all | solution.py:149
  365.3 70.7 %all-to-all-done = bf16[16,2,384,1,128]{4,2,1,3,0:T(8,128)(2,1)} async-done(((bf16[16,2,384,1,128]{4,2,1,3,0:T(8,128)(2,1)}), bf16[16,2,384,1,128]{4,2,1,3,0:T(8,128)(2,1)}, u32[]{:S(2)}, u32[]{:S(2)}) %all-to-all-start) | async-done | bytes 3145760 | tf_op jit(solution)/shard_map/all_to_all | solution.py:149
  436.1 3.8 gather_fusion.1
  (175 shorter events, 98.4 us)
Async XLA Ops:
  7.2 242.5 %copy-start = (bf16[512,2048]{1,0:T(8,128)(2,1)S(1)}, bf16[512,2048]{1,0:T(8,128)(2,1)}, u32[]{:S(2)}) copy-start(bf16[512,2048]{1,0:T(8,128)(2,1)} %param.13) | copy-start | bytes 6291460
  7.2 64.8 %all-gather.3.cloned.1.call-start = ((), (), s32[]{:S(2)}) async-start(), calls=%async_computation.3 | async-start | bytes 4456448 | tf_op jit(solution)/shard_map/all_gather | solution.py:120
  11.5 170.4 %reduce-scatter.3.cloned.1.call-start = ((), (), s32[]{:S(2)}) async-start(), calls=%async_computation.4 | async-start | bytes 8912896 | tf_op jit(solution)/shard_map/reduce_scatter | solution.py:134
  11.5 3.1 copy-start.9
  78.9 7.6 %copy-start.4 = (bf16[8,128,1,64]{1,3,0,2:T(8,128)(2,1)}, bf16[8,128,1,64]{1,3,0,2:T(8,128)(2,1)S(1)}, u32[]{:S(2)}) copy-start(bf16[8,128,1,64]{1,3,0,2:T(8,128)(2,1)S(1)} %get-tuple-element.62) | copy-start | bytes 393220
  78.9 4.3 copy-start.16
  86.5 2.1 copy-start.7
  93.0 88.9 %copy-start.1 = (bf16[64,2048]{1,0:T(8,128)(2,1)S(1)}, bf16[64,2048]{1,0:T(8,128)(2,1)}, u32[]{:S(2)}) copy-start(bf16[64,2048]{1,0:T(8,128)(2,1)} %param.9) | copy-start | bytes 786436
  93.1 92.8 %copy-start.10 = (s32[128]{0:T(128)S(1)}, s32[128]{0:T(128)}, u32[]{:S(2)}) copy-start(s32[128]{0:T(128)} %param.17) | copy-start | bytes 1540
  93.1 149.1 %all-gather.5.cloned.1.call-start = ((), (), s32[]{:S(2)}) async-start(), calls=%async_computation.5 | async-start | bytes 4456448 | tf_op jit(solution)/shard_map/all_gather | solution.py:156
  183.1 0.7 copy-start.2
  184.7 257.9 %reduce-scatter.5.cloned.1.call-start = ((), (), s32[]{:S(2)}) async-start(), calls=%async_computation.6 | async-start | bytes 4456448 | tf_op jit(solution)/shard_map/reduce_scatter | solution.py:162
  185.7 7.4 %copy-start.14 = (s32[8]{0:T(128)}, s32[8]{0:T(128)S(1)}, u32[]{:S(2)}) copy-start(s32[8]{0:T(128)S(1)} %dynamic_slice.12) | copy-start | bytes 100
  185.9 5.8 %copy-start.8 = (s32[4]{0:T(128)S(1)}, s32[4]{0:T(128)}, u32[]{:S(2)}) copy-start(s32[4]{0:T(128)} %constant.165.clone.1) | copy-start | bytes 52
  185.9 7.2 %copy-start.5 = (bf16[8,128,1,64]{1,3,0,2:T(8,128)(2,1)S(1)}, bf16[8,128,1,64]{1,3,0,2:T(8,128)(2,1)}, u32[]{:S(2)}) copy-start(bf16[8,128,1,64]{1,3,0,2:T(8,128)(2,1)} %copy-done.4) | copy-start | bytes 393220
  185.9 7.2 %copy-start.6 = (bf16[8,1,128,1,128]{2,4,0,3,1:T(8,128)(2,1)S(1)}, bf16[8,1,128,1,128]{2,4,0,3,1:T(8,128)(2,1)}, u32[]{:S(2)}) copy-start(bf16[8,1,128,1,128]{2,4,0,3,1:T(8,128)(2,1)} %get-tuple-element.51) | copy-start | bytes 786436
  254.1 1.5 copy-start.13
  349.3 4.1 copy-start.11
  349.3 4.1 copy-start.12
  357.5 7.8 %copy-start.15 = (s32[8]{0:T(128)S(1)}, s32[8]{0:T(128)}, u32[]{:S(2)}) copy-start(s32[8]{0:T(128)} %copy-done.14) | copy-start | bytes 100
  357.5 78.6 %all-to-all-start = ((bf16[16,2,384,1,128]{4,2,1,3,0:T(8,128)(2,1)}), bf16[16,2,384,1,128]{4,2,1,3,0:T(8,128)(2,1)}, u32[]{:S(2)}, u32[]{:S(2)}) async-start(bf16[16,2,384,1,128]{4,2,1,3,0:T(8,128)(2,1)} %fusion.2), calls=%async_computation.2 | async-start | bytes 6291456 | tf_op jit(solution)/shard_map/all_to_all | solution.py:149
  439.8 2.8 copy-start.3
Sparse Core Ops, SparseCore 0:
  11.6 60.3 all-gather.2
  93.2 88.7 reduce-scatter.2
  184.9 57.1 all-gather.4
  254.2 80.8 reduce-scatter.4
where the time goes:
time: 453 us; the launch traced here: 451 us
  waiting for transfers between devices  262 us (58%)
  local copies, waits for them, and re-layouts  103 us (23%)
  other arithmetic  38.4 us (8%)
  matrix products  25.7 us (6%)
  between operations  14 us (3%)
  starting transfers between devices  7.86 us (2%)
    reduce_scatter x1, waiting for transfers between devices, body(): lax.psum_scatter(jnp.dot(picked, w_out.reshape(heads_here * head_size, mo...  88.8 us
    scatter x64, local copies, waits for them, and re-layouts  78.9 us
    all_to_all x1, waiting for transfers between devices, body(): lax.all_to_all(pack_rows(appended, send_from, send_live), 'rep', split_ax...  70.7 us
    all_gather x1, waiting for transfers between devices, body(): lax.all_gather(normed, ('row', 'col'), axis=0, tiled=True)  53.8 us
    all_gather x1, waiting for transfers between devices, body(): lax.all_gather(normed_mid, ('row', 'col'), axis=0, tiled=True)  48.1 us
    scatter x16, other arithmetic  11.8 us
  transfers between devices with their start and end apart: 5, of which 4 were waited for; matrix products, arithmetic and copies ran while one was open for 28% of the time, Pallas kernels for 0%

commit v1 on v0

--- a/solution.py
+++ b/solution.py
@@ -5,6 +5,27 @@
 from jax.sharding import PartitionSpec as P
 
 EPSILON = 1e-05
+
+
+def collect(x, axis, dim):
+    length, index, span = (lax.axis_size(axis), lax.axis_index(axis), x.shape[dim])
+    right = [(i, (i + 1) % length) for i in range(length)]
+    backward = [(i, (i - 1) % length) for i in range(length)]
+    out = jnp.zeros((*x.shape[:dim], length * span, *x.shape[dim + 1 :]), x.dtype)
+    out = lax.dynamic_update_slice_in_dim(out, x, index * span, axis=dim)
+    from_left = from_right = x
+    half = length // 2
+    for step in range(1, half + 1):
+        from_left = lax.ppermute(from_left, axis, right)
+        out = lax.dynamic_update_slice_in_dim(
+            out, from_left, (index - step) % length * span, axis=dim
+        )
+        if step < length - half:
+            from_right = lax.ppermute(from_right, axis, backward)
+            out = lax.dynamic_update_slice_in_dim(
+                out, from_right, (index + step) % length * span, axis=dim
+            )
+    return out
 
 
 def layer_norm(values):
@@ -117,7 +138,7 @@
     inputs = hidden_in.astype(jnp.float32)
     normed = layer_norm(inputs).astype(jnp.bfloat16)
     joined = jnp.dot(
-        lax.all_gather(normed, ("row", "col"), axis=0, tiled=True),
+        collect(normed, ("row", "col"), 0),
         w_qkv.reshape(model_width, heads_here * 3 * head_size),
         preferred_element_type=jnp.float32,
     )

time: 453 us -> 474 us (1.046)
  starting transfers between devices: 7.86 us -> 42.8 us
  waiting for transfers between devices: 262 us -> 236 us
  local copies, waits for them, and re-layouts: 103 us -> 116 us
    all_gather x1 -> x0, waiting for transfers between devices: 53.8 us -> none  [body(): lax.all_gather(normed, ('row', 'col'), axis=0, tiled=True)]
    ppermute x0 -> x15, starting transfers between devices: none -> 35 us  [the longest x7 32.9 us: collect(): from_right = lax.ppermute(from_right, axis, backward)]
    ppermute x0 -> x15, waiting for transfers between devices: none -> 24.5 us  [the longest x8 24.5 us: collect(): from_left = lax.ppermute(from_left, axis, right)]
    dynamic_update_slice x0 -> x15, local copies, waits for them, and re-layouts: none -> 12.8 us  [the longest x8 6.74 us: collect(): lax.dynamic_update_slice_in_dim(out, from_left, (index - step) % length *...]
  transfers between devices with their start and end apart: 5 -> 19, of which waited for: 4 -> 10; matrix products, arithmetic and copies ran while one was open for 28% -> 28% of each run, Pallas kernels for 0% -> 0%
where the time goes in v1:
time: 474 us; the launch traced here: 471 us
  waiting for transfers between devices  236 us (50%)
  local copies, waits for them, and re-layouts  116 us (24%)
  starting transfers between devices  42.8 us (9%)
  other arithmetic  37.5 us (8%)
  matrix products  25.3 us (5%)
  between operations  14 us (3%)
    reduce_scatter x1, waiting for transfers between devices, body(): lax.psum_scatter(jnp.dot(picked, w_out.reshape(heads_here * head_size, mo...  92.1 us
    scatter x64, local copies, waits for them, and re-layouts  75.4 us
    all_to_all x1, waiting for transfers between devices, body(): lax.all_to_all(pack_rows(appended, send_from, send_live), 'rep', split_ax...  70.7 us
    all_gather x1, waiting for transfers between devices, body(): lax.all_gather(normed_mid, ('row', 'col'), axis=0, tiled=True)  48.3 us
    ppermute x7, starting transfers between devices, collect(): from_right = lax.ppermute(from_right, axis, backward)  32.9 us
    ppermute x8, waiting for transfers between devices, collect(): from_left = lax.ppermute(from_left, axis, right)  24.5 us
    scatter x16, other arithmetic  11.8 us
  transfers between devices with their start and end apart: 19, of which 10 were waited for; matrix products, arithmetic and copies ran while one was open for 28% of the time, Pallas kernels for 0%

profile of v1, /device:TPU:1, one launch (start us, length us, event | category | flops | bytes accessed | tf_op | source)
XLA Modules:
  0.0 471.2 jit_solution(7824703296546520298)
XLA Ops:
  15.2 3.7 collective-permute-start.1
  25.5 4.8 %collective-permute-start.3 = (bf16[64,2048]{1,0:T(8,128)(2,1)}, bf16[64,2048]{1,0:T(8,128)(2,1)S(1)}, u32[]{:S(2)}, u32[]{:S(2)}) collective-permute-start(bf16[64,2048]{1,0:T(8,128)(2,1)} %collective-permute-done.1), channel_id=1, source_target_pairs={{0,15},{1,0},{2,1},{3,2},{4,3},{5,4},{6,5},{7,6},{8,7},{9,8},{10,9... | collective-permute-start | bytes 786440 | tf_op jit(solution)/shard_map/ppermute | solution.py:24
  34.2 4.8 %collective-permute-start.5 = (bf16[64,2048]{1,0:T(8,128)(2,1)S(1)}, bf16[64,2048]{1,0:T(8,128)(2,1)S(1)}, u32[]{:S(2)}, u32[]{:S(2)}) collective-permute-start(bf16[64,2048]{1,0:T(8,128)(2,1)S(1)} %collective-permute-done.3), channel_id=1, source_target_pairs={{0,15},{1,0},{2,1},{3,2},{4,3},{5,4},{6,5},{7,6},{8,7},{9,8},{10,9... | collective-permute-start | bytes 786440 | tf_op jit(solution)/shard_map/ppermute | solution.py:24
  42.8 4.8 %collective-permute-start.7 = (bf16[64,2048]{1,0:T(8,128)(2,1)S(1)}, bf16[64,2048]{1,0:T(8,128)(2,1)S(1)}, u32[]{:S(2)}, u32[]{:S(2)}) collective-permute-start(bf16[64,2048]{1,0:T(8,128)(2,1)S(1)} %collective-permute-done.5), channel_id=1, source_target_pairs={{0,15},{1,0},{2,1},{3,2},{4,3},{5,4},{6,5},{7,6},{8,7},{9,8},{10,9... | collective-permute-start | bytes 786440 | tf_op jit(solution)/shard_map/ppermute | solution.py:24
  51.3 4.8 %collective-permute-start.9 = (bf16[64,2048]{1,0:T(8,128)(2,1)S(1)}, bf16[64,2048]{1,0:T(8,128)(2,1)S(1)}, u32[]{:S(2)}, u32[]{:S(2)}) collective-permute-start(bf16[64,2048]{1,0:T(8,128)(2,1)S(1)} %collective-permute-done.7), channel_id=1, source_target_pairs={{0,15},{1,0},{2,1},{3,2},{4,3},{5,4},{6,5},{7,6},{8,7},{9,8},{10,9... | collective-permute-start | bytes 786440 | tf_op jit(solution)/shard_map/ppermute | solution.py:24
  59.9 4.9 %collective-permute-start.11 = (bf16[64,2048]{1,0:T(8,128)(2,1)S(1)}, bf16[64,2048]{1,0:T(8,128)(2,1)S(1)}, u32[]{:S(2)}, u32[]{:S(2)}) collective-permute-start(bf16[64,2048]{1,0:T(8,128)(2,1)S(1)} %collective-permute-done.9), channel_id=1, source_target_pairs={{0,15},{1,0},{2,1},{3,2},{4,3},{5,4},{6,5},{7,6},{8,7},{9,8},{10,9... | collective-permute-start | bytes 786440 | tf_op jit(solution)/shard_map/ppermute | solution.py:24
  66.3 3.1 collective-permute-done.10
  69.4 5.1 %collective-permute-start.13 = (bf16[64,2048]{1,0:T(8,128)(2,1)S(1)}, bf16[64,2048]{1,0:T(8,128)(2,1)S(1)}, u32[]{:S(2)}, u32[]{:S(2)}) collective-permute-start(bf16[64,2048]{1,0:T(8,128)(2,1)S(1)} %collective-permute-done.11), channel_id=1, source_target_pairs={{0,15},{1,0},{2,1},{3,2},{4,3},{5,4},{6,5},{7,6},{8,7},{9,8},{10,9... | collective-permute-start | bytes 786440 | tf_op jit(solution)/shard_map/ppermute | solution.py:24
  76.0 4.0 collective-permute-done.12
  81.5 9.8 %collective-permute-done.14 = bf16[64,2048]{1,0:T(8,128)(2,1)S(1)} collective-permute-done((bf16[64,2048]{1,0:T(8,128)(2,1)S(1)}, bf16[64,2048]{1,0:T(8,128)(2,1)S(1)}, u32[]{:S(2)}, u32[]{:S(2)}) %collective-permute-start.14) | collective-permute-done | bytes 262176 | tf_op jit(solution)/shard_map/ppermute | solution.py:19
  92.0 3.6 convolution_bitcast_fusion
  103.5 3.3 fusion.72
  108.9 4.5 fusion.24
  113.4 92.1 %reduce-scatter.3.cloned.1.call-done = f32[64,2048]{1,0:T(8,128)} async-done(((f32[1024,2048]{1,0:T(8,128)}), f32[64,2048]{1,0:T(8,128)}) %reduce-scatter.3.cloned.1.call-update) | async-done | bytes 524304 | tf_op jit(solution)/shard_map/reduce_scatter | solution.py:155
  209.6 5.4 %copy.153 = bf16[256,8,2,512]{3,1,2,0:T(8,128)(2,1)} copy(bf16[256,8,2,512]{3,2,1,0:T(2,128)(2,1)} %bitcast.121) | data formatting | bytes 8388608
  217.7 48.3 %all-gather.2.cloned.1.call-done = bf16[1024,2048]{1,0:T(8,128)(2,1)} async-done(((bf16[64,2048]{1,0:T(8,128)(2,1)}), bf16[1024,2048]{1,0:T(8,128)(2,1)}) %all-gather.2.cloned.1.call-update) | async-done | bytes 4194320 | tf_op jit(solution)/shard_map/all_gather | solution.py:177
  266.0 7.5 %fusion.75 = f32[1024,1024]{1,0:T(8,128)S(1)} fusion(bf16[1024,2048]{1,0:T(8,128)(2,1)} %all-gather.2.cloned.1.call-done, bf16[2048,1024]{1,0:T(8,128)(2,1)} %bitcast.122), kind=kOutput, calls=%fused_computation.163 | convolution fusion | flops 4294967296 | bytes 12582912 | tf_op jit(solution)/shard_map/dot_general | solution.py:176
  273.5 4.4 convolution_convert_fusion
  279.4 87.4 %while.1 = (s32[]{:T(128)}, bf16[8,2,384,1,128]{4,2,0,3,1:T(8,128)(2,1)}, s32[8,5]{1,0:T(8,128)S(1)}, bf16[8,2,128,1,128]{2,4,0,3,1:T(8,128)(2,1)}, s32[]{:T(128)}, /*index=5*/s32[5]{0:T(128)S(1)}, s32[]{:T(128)}) while((s32[]{:T(128)}, bf16[8,2,384,1,128]{4,2,0,3,1:T(8,128)(2,1)}, s32[8,5]{1,0:T(8,128)S(1)}, bf16[8,2,128,1,128]{2,4,0,3,1:T(8,128)(2,1)}, ...), condition=%wide.while_cond, body=%wide.while_body.sunk | while | flops 32789 | bytes 852227 | solution.py:80
  369.7 4.1 gather_fusion
  373.7 4.0 fusion.2
  377.8 7.5 %all-to-all-start = ((bf16[16,2,384,1,128]{4,2,1,3,0:T(8,128)(2,1)}), bf16[16,2,384,1,128]{4,2,1,3,0:T(8,128)(2,1)}, u32[]{:S(2)}, u32[]{:S(2)}) async-start(bf16[16,2,384,1,128]{4,2,1,3,0:T(8,128)(2,1)} %fusion.2), calls=%async_computation.2 | async-start | bytes 6291456 | tf_op jit(solution)/shard_map/all_to_all | solution.py:170
  385.6 70.7 %all-to-all-done = bf16[16,2,384,1,128]{4,2,1,3,0:T(8,128)(2,1)} async-done(((bf16[16,2,384,1,128]{4,2,1,3,0:T(8,128)(2,1)}), bf16[16,2,384,1,128]{4,2,1,3,0:T(8,128)(2,1)}, u32[]{:S(2)}, u32[]{:S(2)}) %all-to-all-start) | async-done | bytes 3145760 | tf_op jit(solution)/shard_map/all_to_all | solution.py:170
  456.4 3.8 gather_fusion.1
  (218 shorter events, 148.0 us)
Async XLA Ops:
  7.2 266.3 %copy-start = (bf16[512,2048]{1,0:T(8,128)(2,1)S(1)}, bf16[512,2048]{1,0:T(8,128)(2,1)}, u32[]{:S(2)}) copy-start(bf16[512,2048]{1,0:T(8,128)(2,1)} %param.13) | copy-start | bytes 6291460
  7.2 11.7 %copy-start.10 = (s32[128]{0:T(128)S(1)}, s32[128]{0:T(128)}, u32[]{:S(2)}) copy-start(s32[128]{0:T(128)} %param.16) | copy-start | bytes 1540
  7.2 198.3 %reduce-scatter.3.cloned.1.call-start = ((), (), s32[]{:S(2)}) async-start(), calls=%async_computation.3 | async-start | bytes 8912896 | tf_op jit(solution)/shard_map/reduce_scatter | solution.py:155
  13.1 12.4 %collective-permute-start = (bf16[64,2048]{1,0:T(8,128)(2,1)}, bf16[64,2048]{1,0:T(8,128)(2,1)}, u32[]{:S(2)}, u32[]{:S(2)}) collective-permute-start(bf16[64,2048]{1,0:T(8,128)(2,1)} %get-tuple-element.47), channel_id=1, source_target_pairs={{0,1},{1,2},{2,3},{3,4},{4,5},{5,6},{6,7},{7,8},{8,9},{9,10},{10,1... | collective-permute-start | bytes 786440 | tf_op jit(solution)/shard_map/ppermute | solution.py:19
  15.2 10.3 %collective-permute-start.1 = (bf16[64,2048]{1,0:T(8,128)(2,1)}, bf16[64,2048]{1,0:T(8,128)(2,1)}, u32[]{:S(2)}, u32[]{:S(2)}) collective-permute-start(bf16[64,2048]{1,0:T(8,128)(2,1)} %get-tuple-element.47), channel_id=1, source_target_pairs={{0,15},{1,0},{2,1},{3,2},{4,3},{5,4},{6,5},{7,6},{8,7},{9,8},{10,9... | collective-permute-start | bytes 786440 | tf_op jit(solution)/shard_map/ppermute | solution.py:24
  25.5 8.8 %collective-permute-start.2 = (bf16[64,2048]{1,0:T(8,128)(2,1)}, bf16[64,2048]{1,0:T(8,128)(2,1)S(1)}, u32[]{:S(2)}, u32[]{:S(2)}) collective-permute-start(bf16[64,2048]{1,0:T(8,128)(2,1)} %collective-permute-done), channel_id=1, source_target_pairs={{0,1},{1,2},{2,3},{3,4},{4,5},{5,6},{6,7},{7,8},{8,9},{9,10},{10,1... | collective-permute-start | bytes 786440 | tf_op jit(solution)/shard_map/ppermute | solution.py:19
  25.5 8.8 %collective-permute-start.3 = (bf16[64,2048]{1,0:T(8,128)(2,1)}, bf16[64,2048]{1,0:T(8,128)(2,1)S(1)}, u32[]{:S(2)}, u32[]{:S(2)}) collective-permute-start(bf16[64,2048]{1,0:T(8,128)(2,1)} %collective-permute-done.1), channel_id=1, source_target_pairs={{0,15},{1,0},{2,1},{3,2},{4,3},{5,4},{6,5},{7,6},{8,7},{9,8},{10,9... | collective-permute-start | bytes 786440 | tf_op jit(solution)/shard_map/ppermute | solution.py:24
  34.2 8.5 %collective-permute-start.4 = (bf16[64,2048]{1,0:T(8,128)(2,1)S(1)}, bf16[64,2048]{1,0:T(8,128)(2,1)S(1)}, u32[]{:S(2)}, u32[]{:S(2)}) collective-permute-start(bf16[64,2048]{1,0:T(8,128)(2,1)S(1)} %collective-permute-done.2), channel_id=1, source_target_pairs={{0,1},{1,2},{2,3},{3,4},{4,5},{5,6},{6,7},{7,8},{8,9},{9,10},{10,1... | collective-permute-start | bytes 786440 | tf_op jit(solution)/shard_map/ppermute | solution.py:19
  34.2 8.5 %collective-permute-start.5 = (bf16[64,2048]{1,0:T(8,128)(2,1)S(1)}, bf16[64,2048]{1,0:T(8,128)(2,1)S(1)}, u32[]{:S(2)}, u32[]{:S(2)}) collective-permute-start(bf16[64,2048]{1,0:T(8,128)(2,1)S(1)} %collective-permute-done.3), channel_id=1, source_target_pairs={{0,15},{1,0},{2,1},{3,2},{4,3},{5,4},{6,5},{7,6},{8,7},{9,8},{10,9... | collective-permute-start | bytes 786440 | tf_op jit(solution)/shard_map/ppermute | solution.py:24
  39.8 52.2 %copy-start.4 = (bf16[2048,1,384]{0,2,1:T(8,128)(2,1)S(1)}, bf16[2048,1,384]{0,2,1:T(8,128)(2,1)}, u32[]{:S(2)}) copy-start(bf16[2048,1,384]{0,2,1:T(8,128)(2,1)} %copy.49) | copy-start | bytes 4718596
  42.8 8.5 %collective-permute-start.6 = (bf16[64,2048]{1,0:T(8,128)(2,1)S(1)}, bf16[64,2048]{1,0:T(8,128)(2,1)S(1)}, u32[]{:S(2)}, u32[]{:S(2)}) collective-permute-start(bf16[64,2048]{1,0:T(8,128)(2,1)S(1)} %collective-permute-done.4), channel_id=1, source_target_pairs={{0,1},{1,2},{2,3},{3,4},{4,5},{5,6},{6,7},{7,8},{8,9},{9,10},{10,1... | collective-permute-start | bytes 786440 | tf_op jit(solution)/shard_map/ppermute | solution.py:19
  42.8 8.5 %collective-permute-start.7 = (bf16[64,2048]{1,0:T(8,128)(2,1)S(1)}, bf16[64,2048]{1,0:T(8,128)(2,1)S(1)}, u32[]{:S(2)}, u32[]{:S(2)}) collective-permute-start(bf16[64,2048]{1,0:T(8,128)(2,1)S(1)} %collective-permute-done.5), channel_id=1, source_target_pairs={{0,15},{1,0},{2,1},{3,2},{4,3},{5,4},{6,5},{7,6},{8,7},{9,8},{10,9... | collective-permute-start | bytes 786440 | tf_op jit(solution)/shard_map/ppermute | solution.py:24
  51.3 8.5 %collective-permute-start.8 = (bf16[64,2048]{1,0:T(8,128)(2,1)S(1)}, bf16[64,2048]{1,0:T(8,128)(2,1)S(1)}, u32[]{:S(2)}, u32[]{:S(2)}) collective-permute-start(bf16[64,2048]{1,0:T(8,128)(2,1)S(1)} %collective-permute-done.6), channel_id=1, source_target_pairs={{0,1},{1,2},{2,3},{3,4},{4,5},{5,6},{6,7},{7,8},{8,9},{9,10},{10,1... | collective-permute-start | bytes 786440 | tf_op jit(solution)/shard_map/ppermute | solution.py:19
  51.3 8.5 %collective-permute-start.9 = (bf16[64,2048]{1,0:T(8,128)(2,1)S(1)}, bf16[64,2048]{1,0:T(8,128)(2,1)S(1)}, u32[]{:S(2)}, u32[]{:S(2)}) collective-permute-start(bf16[64,2048]{1,0:T(8,128)(2,1)S(1)} %collective-permute-done.7), channel_id=1, source_target_pairs={{0,15},{1,0},{2,1},{3,2},{4,3},{5,4},{6,5},{7,6},{8,7},{9,8},{10,9... | collective-permute-start | bytes 786440 | tf_op jit(solution)/shard_map/ppermute | solution.py:24
  59.9 9.6 %collective-permute-start.10 = (bf16[64,2048]{1,0:T(8,128)(2,1)S(1)}, bf16[64,2048]{1,0:T(8,128)(2,1)S(1)}, u32[]{:S(2)}, u32[]{:S(2)}) collective-permute-start(bf16[64,2048]{1,0:T(8,128)(2,1)S(1)} %collective-permute-done.8), channel_id=1, source_target_pairs={{0,1},{1,2},{2,3},{3,4},{4,5},{5,6},{6,7},{7,8},{8,9},{9,10},{10,1... | collective-permute-start | bytes 786440 | tf_op jit(solution)/shard_map/ppermute | solution.py:19
  59.9 9.6 %collective-permute-start.11 = (bf16[64,2048]{1,0:T(8,128)(2,1)S(1)}, bf16[64,2048]{1,0:T(8,128)(2,1)S(1)}, u32[]{:S(2)}, u32[]{:S(2)}) collective-permute-start(bf16[64,2048]{1,0:T(8,128)(2,1)S(1)} %collective-permute-done.9), channel_id=1, source_target_pairs={{0,15},{1,0},{2,1},{3,2},{4,3},{5,4},{6,5},{7,6},{8,7},{9,8},{10,9... | collective-permute-start | bytes 786440 | tf_op jit(solution)/shard_map/ppermute | solution.py:24
  69.4 10.6 %collective-permute-start.12 = (bf16[64,2048]{1,0:T(8,128)(2,1)S(1)}, bf16[64,2048]{1,0:T(8,128)(2,1)S(1)}, u32[]{:S(2)}, u32[]{:S(2)}) collective-permute-start(bf16[64,2048]{1,0:T(8,128)(2,1)S(1)} %collective-permute-done.10), channel_id=1, source_target_pairs={{0,1},{1,2},{2,3},{3,4},{4,5},{5,6},{6,7},{7,8},{8,9},{9,10},{10,1... | collective-permute-start | bytes 786440 | tf_op jit(solution)/shard_map/ppermute | solution.py:19
  69.4 11.4 %collective-permute-start.13 = (bf16[64,2048]{1,0:T(8,128)(2,1)S(1)}, bf16[64,2048]{1,0:T(8,128)(2,1)S(1)}, u32[]{:S(2)}, u32[]{:S(2)}) collective-permute-start(bf16[64,2048]{1,0:T(8,128)(2,1)S(1)} %collective-permute-done.11), channel_id=1, source_target_pairs={{0,15},{1,0},{2,1},{3,2},{4,3},{5,4},{6,5},{7,6},{8,7},{9,8},{10,9... | collective-permute-start | bytes 786440 | tf_op jit(solution)/shard_map/ppermute | solution.py:24
  80.1 11.2 %collective-permute-start.14 = (bf16[64,2048]{1,0:T(8,128)(2,1)S(1)}, bf16[64,2048]{1,0:T(8,128)(2,1)S(1)}, u32[]{:S(2)}, u32[]{:S(2)}) collective-permute-start(bf16[64,2048]{1,0:T(8,128)(2,1)S(1)} %collective-permute-done.12), channel_id=1, source_target_pairs={{0,1},{1,2},{2,3},{3,4},{4,5},{5,6},{6,7},{7,8},{8,9},{9,10},{10,1... | collective-permute-start | bytes 786440 | tf_op jit(solution)/shard_map/ppermute | solution.py:19
  113.4 96.1 %copy-start.11 = (s32[128]{0:T(128)S(1)}, s32[128]{0:T(128)}, u32[]{:S(2)}) copy-start(s32[128]{0:T(128)} %param.17) | copy-start | bytes 1540
  113.4 152.6 %all-gather.2.cloned.1.call-start = ((), (), s32[]{:S(2)}) async-start(), calls=%async_computation.4 | async-start | bytes 4456448 | tf_op jit(solution)/shard_map/all_gather | solution.py:177
  208.3 254.6 %reduce-scatter.5.cloned.1.call-start = ((), (), s32[]{:S(2)}) async-start(), calls=%async_computation.5 | async-start | bytes 4456448 | tf_op jit(solution)/shard_map/reduce_scatter | solution.py:183
  377.8 7.8 %copy-start.16 = (s32[8]{0:T(128)S(1)}, s32[8]{0:T(128)}, u32[]{:S(2)}) copy-start(s32[8]{0:T(128)} %copy-done.15) | copy-start | bytes 100
  377.8 78.6 %all-to-all-start = ((bf16[16,2,384,1,128]{4,2,1,3,0:T(8,128)(2,1)}), bf16[16,2,384,1,128]{4,2,1,3,0:T(8,128)(2,1)}, u32[]{:S(2)}, u32[]{:S(2)}) async-start(bf16[16,2,384,1,128]{4,2,1,3,0:T(8,128)(2,1)} %fusion.2), calls=%async_computation.2 | async-start | bytes 6291456 | tf_op jit(solution)/shard_map/all_to_all | solution.py:170
  (12 other events, 52.4 us)
Sparse Core Ops, SparseCore 0:
  113.5 91.9 reduce-scatter.2
  208.5 57.4 all-gather.1
  278.0 80.7 reduce-scatter.4
